TPU v7x, 32 devices: a whole 2x2x4 slice. The times are simulated.
32 devices in a mesh: member: 2 (over y), tx: 4 (over z), ty: 4 (over x, core).
Axes of the slice: x: 2, y: 2, z: 4, core: 2. Of those that a mesh axis runs over, the one named last changes fastest.
Arguments:
- tracers: float32 [80, 3, 128, 512], P('member', None, 'tx', 'ty'), parts along dimension 0, may hold values from 0.05 to 2
- velocity: float32 [2, 3, 128, 512], P(None, None, 'tx', 'ty'), may hold values from -0.4 to 0.4
- land_mask: int32 [3, 128, 512], P(None, 'tx', 'ty'), may hold values 0 or 1
- sunlight: float32 [128, 512], P('tx', 'ty'), may hold values from 0.3 to 3
- growth_max: float32 [52], P('member'), parts along dimension 0, may hold values from 0.2 to 1.5
- half_sat: float32 [8, 26], P('member'), parts along dimension 0, may hold values from 0.05 to 1
- light_half: float32 [52], P('member'), parts along dimension 0, may hold values from 0.1 to 1
- graze_max: float32 [20], P('member'), parts along dimension 0, may hold values from 0.2 to 1.5
- graze_half: float32 [20], P('member'), parts along dimension 0, may hold values from 0.2 to 2
- palatable: int32 [20, 26], P('member'), parts along dimension 0, may hold values 0 or 1
- stoichiometry: float32 [4], replicated, may hold values from 0.05 to 1
Outputs:
- updated: float32 [80, 3, 128, 512], P('member', None, 'tx', 'ty'), parts along dimension 0
There are 2 independent parts, one for each index of `member`. A program takes and returns all parts, laid end to end along the dimension named above; an argument that names none is the same for every part. Nothing has to cross between parts.
All inputs are finite; a program needn't handle non-finite values. No bound on the sum of `land_mask` on one device may be relied on, other than what follows from the above.
Results may differ from a plain program's by a relative error of at most 0.000064.
Values sent between devices are 32-bit elements; how exact they have to be, the bound alone decides.
No kernel may reach another device: no remote copies, remote signals or barrier semaphores. Data moves between devices by JAX's collectives and lax.ppermute only.
A program may use at most 64 MiB of HBM per device.

v0:
```python
import jax
import jax.numpy as jnp
from jax import lax
from jax.experimental import pallas as pl
from jax.experimental.pallas import tpu as pltpu
from jax.sharding import PartitionSpec as P


NNUT = 4
NPHY = 26
DEPTH = 12

plankton_mortality = 0.05
grazer_mortality = 0.3
assimilation = 0.3
attenuation = 0.4

VMEM = pl.BlockSpec(memory_space=pltpu.VMEM)
SMEM = pl.BlockSpec(memory_space=pltpu.SMEM)
ANY = pl.BlockSpec(memory_space=pl.ANY)
HBM = pl.BlockSpec(memory_space=pltpu.HBM)


def in_vmem(array):
    return pltpu.with_memory_space_constraint(array, pltpu.VMEM)


def in_hbm(array):
    return pltpu.with_memory_space_constraint(array, pltpu.HBM)


def call(kernel, outs, specs, scratch=(), flops=0, bytes_accessed=0, limit=8 << 20, **more):
    return pl.pallas_call(
        kernel,
        out_shape=outs,
        in_specs=specs,
        scratch_shapes=list(scratch),
        cost_estimate=pl.CostEstimate(flops=flops, bytes_accessed=bytes_accessed, transcendentals=0),
        compiler_params=pltpu.CompilerParams(vmem_limit_bytes=limit),
        **more,
    )


class Deferred:
    def __init__(self, depth):
        self.depth, self.queue = depth, []

    def put(self, ref, index, value):
        self.queue.append((ref, index, value))
        if len(self.queue) > self.depth:
            self.pop()

    def pop(self):
        ref, index, value = self.queue.pop(0)
        ref[index] = value

    def flush(self):
        while self.queue:
            self.pop()


def diet_matrices(palatable, to_grazers, to_plants):
    f32, bf16 = jnp.float32, jnp.bfloat16
    grazers = palatable.shape[0]

    def picks(shape, dim, period):
        index = lax.broadcasted_iota(jnp.int32, shape, dim)
        index = jnp.where(index < period, index, index - period)
        other = lax.broadcasted_iota(jnp.int32, shape, 1 - dim)
        return jnp.where((index >> 3) == other, 1.0, 0.0).astype(bf16)

    def spread(left, middle, right, transposed):
        dims = (((1,), (1 if transposed else 0,)), ((), ()))
        part = lax.dot_general(left, middle, dims, preferred_element_type=f32).astype(bf16)
        whole = jnp.dot(part, right, preferred_element_type=f32)
        row = lax.broadcasted_iota(jnp.int32, whole.shape, 0) & 7
        col = lax.broadcasted_iota(jnp.int32, whole.shape, 1) & 7
        return jnp.where(row == col, whole, 0.0).astype(bf16)

    eats = palatable[...].astype(f32).astype(bf16)
    rows_z, rows_k = 8 * grazers, 8 * NPHY
    to_grazers[...] = spread(
        picks((rows_z, grazers), 0, rows_z), eats, picks((NPHY, 2 * rows_k), 1, rows_k), False
    )
    to_plants[...] = spread(
        picks((rows_k, NPHY), 0, rows_k), eats, picks((grazers, 2 * rows_z), 1, rows_z), True
    )


def pack_rows(tracers, velocity, mask, first, last, edge, sems):
    count, length = tracers.shape[0], tracers.shape[1]
    levels = mask.shape[0]
    forcing = pl.ds(count, levels)
    copies = []
    for side, (out, rows, row) in enumerate(
        ((first, pl.ds(0, 2), pl.ds(0, 1)), (last, pl.ds(length - 2, 2), pl.ds(length - 1, 1)))
    ):
        copies += [
            pltpu.make_async_copy(tracers.at[:, rows], out.at[pl.ds(0, count)], sems.at[side, 0]),
            pltpu.make_async_copy(
                velocity.at[0, :, row], out.at[forcing, pl.ds(0, 1)], sems.at[side, 1]
            ),
            pltpu.make_async_copy(mask.at[:, row], edge.at[side], sems.at[side, 2]),
        ]
    for copy in copies:
        copy.start()
    for out in (first, last):
        out[count + levels :] = jnp.zeros_like(out[count + levels :])
    for copy in copies:
        copy.wait()
    for side, out in enumerate((first, last)):
        out[forcing, pl.ds(1, 1)] = edge[side].astype(jnp.float32)


def ecology(
    tracers,
    mask,
    sunlight,
    palatable,
    growth_max,
    half_sat,
    light_half,
    graze_max,
    graze_half,
    stoichiometry,
    _,
    tendency,
    to_grazers,
    to_plants,
):
    count, levels, length, lanes = tracers.shape
    grazers = count - NNUT - NPHY
    f32, bf16 = jnp.float32, jnp.bfloat16
    plants = pl.ds(NNUT, NPHY)

    diet_matrices(palatable, to_grazers, to_plants)

    def split(values):
        wide = jnp.concatenate([v.reshape(-1, lanes) for v in values], axis=1)
        high = wide.astype(bf16)
        return jnp.concatenate([high, (wide - high.astype(f32)).astype(bf16)], axis=0)

    def entry(wide, n):
        part = wide[8 * n : 8 * n + 8]
        return jnp.concatenate([part[:, :lanes], part[:, lanes:]], axis=0)

    def level_step(level, carry):
        depth = jnp.exp(jnp.full((8, 128), -attenuation * (level + 0.5), f32))[0:1, 0:1]
        for start in range(0, length, 16):
            rows = pl.ds(start, 16)
            halves = (pl.ds(start, 8), pl.ds(start + 8, 8))
            available = jnp.dot(
                to_grazers[...],
                split([tracers[plants, level, half] for half in halves]),
                preferred_element_type=f32,
            )
            wet = mask[level, rows].astype(f32)
            recycled = jnp.zeros((16, lanes), f32)
            rates = []
            later = Deferred(DEPTH)

            def add(t, change):
                later.put(tendency, (t, level, rows), tendency[t, level, rows] + wet * change)

            for z in range(grazers):
                grazer = tracers[NNUT + NPHY + z, level, rows]
                prey = entry(available, z)
                rate = graze_max[z] * grazer / (graze_half[z] + prey)
                ingested = rate * prey
                loss = grazer_mortality * grazer * grazer
                add(NNUT + NPHY + z, assimilation * ingested - loss)
                recycled = recycled + (loss + (1.0 - assimilation) * ingested)
                rates.append(rate)
            pressure = jnp.dot(
                to_plants[...],
                split([jnp.concatenate([r[n : n + 8] for r in rates], axis=0) for n in (0, 8)]),
                preferred_element_type=f32,
            )
            darkness = 1.0 / (sunlight[rows] * depth)
            scarcity = [1.0 / tracers[j, level, rows] for j in range(NNUT)]
            for k in range(NPHY):
                plant = tracers[NNUT + k, level, rows]
                worst = half_sat[0, k] * scarcity[0]
                for j in range(1, NNUT):
                    worst = jnp.maximum(worst, half_sat[j, k] * scarcity[j])
                growth = (growth_max[k] * plant) / (
                    (1.0 + worst) * (1.0 + light_half[k] * darkness)
                )
                recycled = recycled + (plankton_mortality * plant - growth)
                add(NNUT + k, growth - plant * (entry(pressure, k) + plankton_mortality))
            for j in range(NNUT):
                add(j, stoichiometry[j] * recycled)
            later.flush()
        return carry

    for level in range(levels):
        level_step(level, 0)


def face_terms(u):
    up, down = jnp.maximum(u, 0.0), jnp.minimum(u, 0.0)
    return (
        up * (-1.0 / 6.0),
        up * (5.0 / 6.0) + down * (1.0 / 3.0),
        up * (1.0 / 3.0) + down * (5.0 / 6.0),
        down * (-1.0 / 6.0),
    )


def stencil(lower, upper):
    a0, b0, d0, e0 = face_terms(lower)
    a1, b1, d1, e1 = face_terms(upper)
    return a0, b0 - a1, 1.0 + (upper - lower) + d0 - b1, e0 - d1, -e1


def row_weights(velocity, mask, level, wet_before, wet_after, flow_after):
    length, lanes = mask.shape[1:]
    rows = lax.broadcasted_iota(jnp.int32, (length, lanes), 0)
    wet = mask[level].astype(jnp.float32)
    wet_up = jnp.where(rows == 0, wet_before, pltpu.roll(wet, 1, 0))
    lower = velocity[0, level] * (wet_up * wet)
    upper = jnp.where(
        rows == length - 1, flow_after * (wet * wet_after), pltpu.roll(lower, length - 1, 0)
    )
    return stencil(lower, upper)


def column_weights(velocity, mask, level, here):
    lanes = mask.shape[2]
    lane = lax.broadcasted_iota(jnp.int32, (8, lanes), 1)
    wet = mask[level, here].astype(jnp.float32)
    lower = jnp.where(lane == 0, 0.0, velocity[1, level, here] * wet * pltpu.roll(wet, 1, 1))
    upper = pltpu.roll(lower, lanes - 1, 1)
    wm2, wm1, w0, wp1, wp2 = stencil(lower, upper)
    return (
        jnp.where(lane < 2, 0.0, wm2),
        jnp.where(lane < 1, 0.0, wm1),
        w0,
        jnp.where(lane > lanes - 2, 0.0, wp1),
        jnp.where(lane > lanes - 3, 0.0, wp2),
    )


def sweep_across(centre, weights):
    wm2, wm1, w0, wp1, wp2 = weights
    lanes = centre.shape[1]
    return (
        w0 * centre
        + (wm1 * pltpu.roll(centre, 1, 1) + wm2 * pltpu.roll(centre, 2, 1))
        + (wp1 * pltpu.roll(centre, lanes - 1, 1) + wp2 * pltpu.roll(centre, lanes - 2, 1))
    )


def swaps(size):
    return size % 2 == 0


def first_is_right():
    size = lax.axis_size("ty")
    if not swaps(size):
        return True, True
    even = lax.axis_index("ty") % 2 == 0
    return even, jnp.logical_not(even)


def pick(choice, a, b):
    return (a if choice else b) if isinstance(choice, bool) else jnp.where(choice, a, b)


class Packer:
    def __init__(self, count, velocity, mask, level, here):
        wet = mask[level, here].astype(jnp.float32)
        lane = lax.broadcasted_iota(jnp.int32, wet.shape, 1)
        self.slot = lane // 2
        self.left = self.right = jnp.zeros_like(wet)
        self.add(count, jnp.where(lane < 2, velocity[1, level, here] * wet, wet))

    def add(self, t, value):
        turned = pltpu.roll(value, 2 * t + 2, 1)
        self.right = jnp.where(self.slot == t, turned, self.right)
        self.left = jnp.where(self.slot == t + 1, turned, self.left)


def interior(
    tracers, velocity, mask, partial, pack_first, pack_second, columns, swept, weights
):
    count, levels, length, lanes = tracers.shape
    zero = jnp.zeros((1, lanes), jnp.float32)
    for level in range(levels):
        for n, w in enumerate(row_weights(velocity, mask, level, zero, zero, zero)):
            weights[n, level] = w
        for block in range(length // 8):
            here = pl.ds(8 * block, 8)
            for n, w in enumerate(column_weights(velocity, mask, level, here)):
                columns[n, level, here] = w
    to_right, _ = first_is_right()
    blocks = length // 8 - 2

    def step(index, carry):
        level = index // blocks
        begin = 8 * (1 + index % blocks)
        here = pl.ds(begin, 8)
        wm2, wm1, w0, wp1, wp2 = [weights[n, level, here] for n in range(5)]
        sideways = [columns[n, level, here] for n in range(5)]
        packer = Packer(count, velocity, mask, level, here)
        later = Deferred(DEPTH)
        for t in range(count):
            at = lambda offset: tracers[t, level, pl.ds(begin + offset, 8)]
            value = w0 * at(0) + (wm1 * at(-1) + wm2 * at(-2)) + (wp1 * at(1) + wp2 * at(2))
            packer.add(t, value)
            later.put(partial, (t, level, here), sweep_across(value, sideways))
        later.flush()
        pack_first[level, here] = pick(to_right, packer.right, packer.left)
        pack_second[level, here] = pick(to_right, packer.left, packer.right)
        return carry

    def clear(level, carry):
        for t in range(count):
            partial[t, level, 0:8] = jnp.zeros((8, lanes), jnp.float32)
            partial[t, level, length - 8 : length] = jnp.zeros((8, lanes), jnp.float32)
        return carry

    lax.fori_loop(0, levels, clear, 0)
    for index in range(levels * blocks):
        step(index, 0)
    sweep_border_inside(tracers, weights, swept)


def edge_rows(weights, side):
    wm2, wm1, w0, wp1, wp2 = weights
    row = lax.broadcasted_iota(jnp.int32, w0.shape, 0)
    if side == 0:
        near, far = row < 1, row < 2
        inside = (jnp.where(far, 0.0, wm2), jnp.where(near, 0.0, wm1), w0, wp1, wp2)
        return inside, (jnp.where(far, wm2, 0.0), jnp.where(near, wm1, 0.0))
    near, far = row > 6, row > 5
    inside = (wm2, wm1, w0, jnp.where(near, 0.0, wp1), jnp.where(far, 0.0, wp2))
    return inside, (jnp.where(far, wp2, 0.0), jnp.where(near, wp1, 0.0))


def sweep_border_inside(tracers, weights, swept):
    count, levels, length, _ = tracers.shape
    for level in range(levels):
        for side, first in enumerate((0, length - 8)):
            here = pl.ds(first, 8)
            (wm2, wm1, w0, wp1, wp2), _ = edge_rows([weights[n, level, here] for n in range(5)], side)
            later = Deferred(DEPTH)
            for t in range(count):
                centre = tracers[t, level, here]

                def at(offset):
                    if (offset < 0) == (side == 0):
                        return pltpu.roll(centre, -offset % 8, 0)
                    return tracers[t, level, pl.ds(first + offset, 8)]

                value = w0 * centre + (wm1 * at(-1) + wm2 * at(-2)) + (wp1 * at(1) + wp2 * at(2))
                later.put(swept, (t, level, pl.ds(8 * side, 8)), value)
            later.flush()


def border(
    tracers,
    velocity,
    mask,
    before,
    after,
    _partial,
    _first,
    _second,
    _swept,
    swept,
    pack_first,
    pack_second,
    through,
):
    count, levels, length, lanes = tracers.shape
    zero = jnp.zeros((1, lanes), jnp.float32)
    to_right, _ = first_is_right()
    for level in range(levels):
        row = lambda ref, field: ref[pl.ds(2 * (count * levels + level) + field, 1)]
        opened = row_weights(velocity, mask, level, row(before, 1), row(after, 1), row(after, 0))
        closed = row_weights(velocity, mask, level, zero, zero, zero)
        for side, first in enumerate((0, length - 8)):
            here, there = pl.ds(first, 8), pl.ds(8 * side, 8)
            inside, (z2, z1) = edge_rows([w[first : first + 8] for w in opened], side)
            shut, _ = edge_rows([w[first : first + 8] for w in closed], side)
            own = inside[2] - shut[2]
            inward = inside[3] - shut[3] if side == 0 else inside[1] - shut[1]
            packer = Packer(count, velocity, mask, level, here)
            later = Deferred(DEPTH)
            for t in range(count):
                group = 2 * (t * levels + level)
                if side == 0:
                    beyond = z2 * before[pl.ds(group, 8)] + z1 * before[pl.ds(group + 1, 8)]
                elif group < 7:
                    outside = after[pl.ds(group, 8)]
                    beyond = z2 * pltpu.roll(outside, 6, 0) + z1 * pltpu.roll(outside, 7, 0)
                else:
                    beyond = z2 * after[pl.ds(group - 6, 8)] + z1 * after[pl.ds(group - 7, 8)]
                next_in = tracers[t, level, pl.ds(first + (1 if side == 0 else -1), 8)]
                value = (swept[t, level, there] + beyond) + (
                    own * tracers[t, level, here] + inward * next_in
                )
                later.put(swept, (t, level, there), value)
                packer.add(t, value)
            later.flush()
            pack_first[level, here] = pick(to_right, packer.right, packer.left)
            pack_second[level, here] = pick(to_right, packer.left, packer.right)


PREPARED = 8


def border_across(swept, velocity, mask, columns, my_first, my_second, _, partial, ready):
    count, levels, _, lanes = swept.shape
    length = mask.shape[1]
    place, size = lax.axis_index("ty"), lax.axis_size("ty")
    has_left = jnp.where(place > 0, 1.0, 0.0)
    has_right = jnp.where(place < size - 1, 1.0, 0.0)
    col = lambda value, n: jnp.broadcast_to(value[:, n : n + 1], value.shape)

    def step(index, carry):
        level, side = index // 2, index % 2
        here = pl.ds(side * (length - 8), 8)
        sideways = [columns[n, level, here] for n in range(5)]
        later = Deferred(DEPTH)
        for t in range(count):
            value = swept[t, level, pl.ds(8 * side, 8)]
            later.put(partial, (t, level, here), partial[t, level, here] + sweep_across(value, sideways))
        later.flush()
        return carry

    for index in range(2 * levels):
        step(index, 0)

    def prepare(level, carry):
        for block in range(length // 8):
            here = pl.ds(8 * block, 8)
            wet = mask[level, here].astype(jnp.float32)
            flow = velocity[1, level, here]
            opened = flow * wet * pltpu.roll(wet, 1, 1)
            to_right, _ = first_is_right()
            first, second = my_first[level, here], my_second[level, here]
            left, right = pick(to_right, second, first), pick(to_right, first, second)
            arrays = (
                col(flow * wet, 0) * has_left,
                col(wet, lanes - 1) * has_right,
                face_terms(col(opened, 1))[0] * has_left,
                face_terms(col(opened, lanes - 1))[3] * has_right,
                pltpu.roll(left, lanes - 2, 1),
                pltpu.roll(left, lanes - 3, 1),
                pltpu.roll(right, lanes - 2, 1),
                pltpu.roll(right, lanes - 1, 1),
            )
            for n, array in enumerate(arrays):
                ready[n, level, here] = array
        return carry

    for level in range(levels):
        prepare(level, 0)


def finish(ready, first, second, _, done, updated, even, odd, sems):
    count, levels, length, lanes = done.shape
    blocks = length // 8
    lane = lax.broadcasted_iota(jnp.int32, (8, lanes), 1)
    is_odd = lane % 2 == 1
    slot_odd = (lane // 2) % 2 == 1
    col = lambda value, n: jnp.broadcast_to(value[:, n : n + 1], value.shape)

    def level_step(level, carry):
        for block in range(blocks):
            here = pl.ds(8 * block, 8)
            open_low, open_high, a1, e127, s0, s1, s127, s126 = (
                ready[n, level, here] for n in range(PREPARED)
            )
            _, of_left = first_is_right()
            one, two = first[level, here], second[level, here]
            left = pick(of_left, one, two)
            right = pltpu.roll(pick(of_left, two, one), lanes - 4, 1)
            u0 = open_low * col(left, 2 * count + 1)
            u128 = open_high * col(right, 2 * count - 2)
            a0, b0, d0, e0 = face_terms(u0)
            a128, b128, d128, e128 = face_terms(u128)
            low = jnp.where(is_odd, a1, a0) * left + jnp.where(
                is_odd,
                0.0,
                (b0 - a1) * pltpu.roll(left, lanes - 1, 1) + ((d0 - u0) * s0 + e0 * s1),
            )
            high = jnp.where(
                is_odd,
                (e127 - d128) * pltpu.roll(right, 1, 1) + ((u128 - b128) * s127 - a128 * s126),
                0.0,
            ) - jnp.where(is_odd, e128, e127) * right
            even[level, here] = jnp.where(slot_odd, high, low)
            odd[level, here] = jnp.where(slot_odd, low, high)
        return carry

    for level in range(levels):
        level_step(level, 0)
    outer = (lane < 2) | (lane > lanes - 3)
    step = 4 if count % 4 == 0 else 2

    def copy(chunk):
        part = pl.ds(chunk * step, step)
        return pltpu.make_async_copy(done.at[part], updated.at[part], sems.at[chunk])

    def add(chunk, carry):
        start = chunk * step
        turns = [(lanes - 2 * (start + n)) % lanes for n in range(step)]
        later = Deferred(2 * DEPTH)
        for n in range(step):
            for level in range(levels):
                for block in range(blocks):
                    here = pl.ds(8 * block, 8)
                    edge = pltpu.roll((even, odd)[n % 2][level, here], turns[n], 1)
                    at = (start + n, level, here)
                    later.put(done, at, done[at] + jnp.where(outer, edge, 0.0))
        later.flush()
        copy(chunk).start()
        return carry

    def wait(chunk, carry):
        copy(chunk).wait()
        return carry

    for chunk in range(count // step):
        add(chunk, 0)
    lax.fori_loop(0, count // step, wait, 0)


def shards(
    tracers,
    velocity,
    land_mask,
    sunlight,
    growth_max,
    half_sat,
    light_half,
    graze_max,
    graze_half,
    palatable,
    stoichiometry,
):
    f32 = jnp.float32
    count, levels, length, lanes = tracers.shape
    tx, ty = lax.axis_size("tx"), lax.axis_size("ty")
    up = lambda n: [(i, (i + 1) % n) for i in range(n)]
    down = lambda n: [((i + 1) % n, i) for i in range(n)]
    cells = count * levels * length * lanes

    assert length % 16 == 0 and count % 2 == 0 and 2 * count + 4 <= lanes
    groups = -(-(count * levels + levels + 1) // 4) * 4
    row_message = pltpu.VMEM((groups, 2, 1, lanes), f32)
    grazers = count - NNUT - NPHY
    first, last = call(
        pack_rows,
        (row_message, row_message),
        [HBM, HBM, HBM],
        scratch=[pltpu.VMEM((2, levels, 1, 1, lanes), jnp.int32), pltpu.SemaphoreType.DMA((2, 3))],
        bytes_accessed=8 * groups * lanes,
        limit=2 << 20,
    )(
        in_hbm(tracers.reshape(count * levels, length, 1, lanes)),
        in_hbm(velocity.reshape(2, levels, length, 1, lanes)),
        in_hbm(land_mask.reshape(levels, length, 1, lanes)),
    )
    first, last = first.reshape(2 * groups, lanes), last.reshape(2 * groups, lanes)
    before = lax.ppermute(last, "tx", up(tx))
    after = lax.ppermute(first, "tx", down(tx))

    held, flow, mask = in_vmem(tracers), in_vmem(velocity), in_vmem(land_mask)
    field = pltpu.VMEM(tracers.shape, f32)
    columns = pltpu.VMEM((levels, length, lanes), f32)
    stencils = pltpu.VMEM((5, levels, length, lanes), f32)
    ends = pltpu.VMEM((count, levels, 16, lanes), f32)
    partial, pack_first, pack_second, sideways, swept = call(
        interior,
        (field, columns, columns, stencils, ends),
        [VMEM] * 3,
        scratch=[stencils],
        flops=20 * cells,
        bytes_accessed=8 * cells,
        limit=2 << 20,
    )(held, flow, mask)
    partial = call(
        ecology,
        field,
        [VMEM] * 4 + [SMEM] * 6 + [VMEM],
        scratch=[
            pltpu.VMEM((8 * grazers, 16 * NPHY), jnp.bfloat16),
            pltpu.VMEM((8 * NPHY, 16 * grazers), jnp.bfloat16),
        ],
        flops=40 * cells,
        bytes_accessed=8 * cells,
        limit=2 << 20,
        input_output_aliases={10: 0},
    )(
        held,
        mask,
        in_vmem(sunlight),
        in_vmem(palatable),
        growth_max,
        half_sat,
        light_half,
        graze_max,
        graze_half,
        stoichiometry,
        partial,
    )
    swept, pack_first, pack_second, partial = call(
        border,
        (ends, columns, columns, field),
        [VMEM] * 5 + [ANY] * 3 + [VMEM],
        out_specs=[VMEM] * 3 + [ANY],
        flops=10 * cells,
        bytes_accessed=8 * cells,
        limit=2 << 20,
        input_output_aliases={5: 3, 6: 1, 7: 2, 8: 0},
    )(held, flow, mask, in_vmem(before), in_vmem(after), partial, pack_first, pack_second, swept)
    pair = lambda n, odd: [p for i in range(odd, n, 2) for p in ((i, (i + 1) % n), ((i + 1) % n, i))]
    turns = (pair(ty, 0), pair(ty, 1)) if swaps(ty) else (up(ty), down(ty))
    from_first = lax.ppermute(pack_first, "ty", turns[0])
    from_second = lax.ppermute(pack_second, "ty", turns[1])
    partial, ready = call(
        border_across,
        (field, pltpu.VMEM((PREPARED, levels, length, lanes), f32)),
        [VMEM] * 7,
        flops=10 * cells,
        bytes_accessed=6 * cells,
        limit=2 << 20,
        input_output_aliases={6: 0},
    )(swept, flow, mask, sideways, pack_first, pack_second, partial)
    return call(
        finish,
        (field, jax.ShapeDtypeStruct(tracers.shape, f32)),
        [VMEM] * 4,
        out_specs=[VMEM, HBM],
        input_output_aliases={3: 0},
        scratch=[
            pltpu.VMEM((levels, length, lanes), f32),
            pltpu.VMEM((levels, length, lanes), f32),
            pltpu.SemaphoreType.DMA((count // 2,)),
        ],
        flops=4 * cells,
        bytes_accessed=8 * cells,
        limit=2 << 20,
    )(ready, in_vmem(from_first), in_vmem(from_second), partial)[1]


def solution(mesh):
    return jax.shard_map(
        shards,
        mesh=mesh,
        in_specs=(
            P("member", None, "tx", "ty"),
            P(None, None, "tx", "ty"),
            P(None, "tx", "ty"),
            P("tx", "ty"),
            P("member"),
            P("member", None),
            P("member"),
            P("member"),
            P("member"),
            P("member", None),
            P(),
        ),
        out_specs=P("member", None, "tx", "ty"),
        check_vma=False,
    )
```

profile of v0, /device:TPU:0, one launch (start us, length us, event | category | flops | bytes accessed | tf_op | source)
XLA Modules:
  0.0 19.1 jit_solution(9483333289467199395)
XLA Ops:
  0.0 0.0 copy-start
  0.0 0.0 copy-start.5
  0.0 0.0 copy-start.6
  0.0 0.0 copy-start.7
  0.0 0.0 copy-start.8
  0.1 0.0 copy-start.9
  0.1 0.0 copy-start.10
  0.1 1.2 %shard_map.109 = (f32[124,2,1,128]{3,2,1,0:T(1,128)S(1)}, f32[124,2,1,128]{3,2,1,0:T(1,128)S(1)}) custom-call(f32[120,32,1,128]{3,2,1,0:T(1,128)} %bitcast.5, f32[2,3,32,1,128]{4,3,2,1,0:T(1,128)} %bitcast.6, s32[3,32,1,128]{3,2,1,0:T(1,128)} %bitcast.7), custom_call_target="tpu_custom_call" | custom-call | bytes 126976 | tf_op jit(solution)/shard_map/pallas_call | solution.py:556
  1.3 5.1 %collective-permute-start.1 = (f32[248,128]{1,0:T(8,128)S(1)}, f32[248,128]{1,0:T(8,128)S(1)}, u32[]{:S(2)}, u32[]{:S(2)}) collective-permute-start(f32[248,128]{1,0:T(8,128)S(1)} %bitcast.9), channel_id=1, source_target_pairs={{4,0},{8,4},{12,8},{0,12},{5,1},{9,5},{13,9},{1,13},{6,2},{10,6},{... | collective-permute-start | bytes 380936 | tf_op jit(solution)/shard_map/ppermute | solution.py:570
  6.4 0.0 collective-permute-start
  6.4 0.0 copy-done
  6.4 0.0 copy-done.1
  6.4 0.0 copy-done.2
  6.4 1.9 %shard_map.110 = (f32[40,3,32,128]{3,2,1,0:T(8,128)S(1)}, f32[3,32,128]{2,1,0:T(8,128)S(1)}, f32[3,32,128]{2,1,0:T(8,128)S(1)}, f32[5,3,32,128]{3,2,1,0:T(8,128)S(1)}, f32[40,3,16,128]{3,2,1,0:T(8,128)S(1)}) custom-call(f32[40,3,32,128]{3,2,1,0:T(8,128)S(1)} %copy-done, f32[2,3,32,128]{3,2,1,0:T(8,128)S(1)} %copy-done.1, s32[3,32,128]{2,1,0:T(8,128)S(1)} %copy-done.2), custom_call_target="tpu_custom_call" | custom-call | flops 9830400 | bytes 3932160 | tf_op jit(solution)/shard_map/pallas_call | solution.py:577
  8.3 0.0 copy-done.3
  8.3 0.0 copy-done.4
  8.3 0.0 copy-done.5
  8.4 0.0 copy-done.6
  8.4 0.0 copy-done.7
  8.4 0.0 copy-done.8
  8.4 0.0 copy-done.9
  8.4 0.0 copy-done.10
  8.4 2.5 %shard_map.111._partial = f32[40,3,32,128]{3,2,1,0:T(8,128)S(1)} custom-call(f32[40,3,32,128]{3,2,1,0:T(8,128)S(1)} %copy-done, s32[3,32,128]{2,1,0:T(8,128)S(1)} %copy-done.2, f32[32,128]{1,0:T(8,128)S(1)} %copy-done.3, s32[10,26]{1,0:T(8,128)S(1)} %copy-done.4, f32[26]{0:T(128)S(1)} %copy-done.6, ...), custom_call_target="tpu_custom_call", output_to_operand_aliasing={{}: (10, {})} | custom-call | flops 19660800 | bytes 3932160 | tf_op jit(solution)/shard_map/pallas_call | solution.py:586
  10.9 0.0 collective-permute-done.1.after
  10.9 2.2 %collective-permute-done.before = f32[248,128]{1,0:T(8,128)S(1)} collective-permute-done((f32[248,128]{1,0:T(8,128)S(1)}, f32[248,128]{1,0:T(8,128)S(1)}, u32[]{:S(2)}, u32[]{:S(2)}) %collective-permute-start) | collective-permute-done | bytes 127008 | tf_op jit(solution)/shard_map/ppermute | solution.py:569
  13.1 0.6 %shard_map.112 = (f32[40,3,16,128]{3,2,1,0:T(8,128)S(1)}, f32[3,32,128]{2,1,0:T(8,128)S(1)}, f32[3,32,128]{2,1,0:T(8,128)S(1)}, f32[40,3,32,128]{3,2,1,0:T(8,128)S(1)}) custom-call(f32[40,3,32,128]{3,2,1,0:T(8,128)S(1)} %copy-done, f32[2,3,32,128]{3,2,1,0:T(8,128)S(1)} %copy-done.1, ...), custom_call_target="tpu_custom_call", output_to_operand_aliasing={{3}: (5, {}), {1}: (6, {}), {2}: (7, {}), {0}: (8, {})} | custom-call | flops 4915200 | bytes 3932160 | tf_op jit(solution)/shard_map/pallas_call | solution.py:611
  13.7 0.1 collective-permute-start.2
  13.8 1.6 %collective-permute-start.3 = (f32[3,32,128]{2,1,0:T(8,128)S(1)}, f32[3,32,128]{2,1,0:T(8,128)S(1)}, u32[]{:S(2)}, u32[]{:S(2)}) collective-permute-start(f32[3,32,128]{2,1,0:T(8,128)S(1)} %get-tuple-element.28.my_second), channel_id=1, source_target_pairs={{1,2},{2,1},{3,0},{0,3},{5,6},{6,5},{7,4},{4,7},{9,10},{10,9},{11,... | collective-permute-start | bytes 147464 | tf_op jit(solution)/shard_map/ppermute | solution.py:624
  15.4 1.5 %shard_map.113 = (f32[40,3,32,128]{3,2,1,0:T(8,128)S(1)}, f32[8,3,32,128]{3,2,1,0:T(8,128)S(1)}) custom-call(f32[40,3,16,128]{3,2,1,0:T(8,128)S(1)} %get-tuple-element.25.swept, f32[2,3,32,128]{3,2,1,0:T(8,128)S(1)} %copy-done.1, s32[3,32,128]{2,1,0:T(8,128)S(1)} %copy-done.2, ...), custom_call_target="tpu_custom_call", output_to_operand_aliasing={{0}: (6, {})} | custom-call | flops 4915200 | bytes 2949120 | tf_op jit(solution)/shard_map/pallas_call | solution.py:625
  16.9 0.0 collective-permute-done.2.first
  16.9 0.5 %collective-permute-done.3.second = f32[3,32,128]{2,1,0:T(8,128)S(1)} collective-permute-done((f32[3,32,128]{2,1,0:T(8,128)S(1)}, f32[3,32,128]{2,1,0:T(8,128)S(1)}, u32[]{:S(2)}, u32[]{:S(2)}) %collective-permute-start.3) | collective-permute-done | bytes 49184 | tf_op jit(solution)/shard_map/ppermute | solution.py:624
  17.4 1.7 %shard_map.114 = (f32[40,3,32,128]{3,2,1,0:T(8,128)S(1)}, f32[40,3,32,128]{3,2,1,0:T(8,128)}) custom-call(f32[8,3,32,128]{3,2,1,0:T(8,128)S(1)} %get-tuple-element.30.ready, f32[3,32,128]{2,1,0:T(8,128)S(1)} %collective-permute-done.2.first, f32[3,32,128]{2,1,0:T(8,128)S(1)} %collective-permute-done.3.second, ...), custom_call_target="tpu_custom_call", output_to_operand_aliasing={{0}: (3, {})} | custom-call | flops 1966080 | bytes 3932160 | tf_op jit(solution)/shard_map/pallas_call | solution.py:634
  (4 shorter events, 0.0 us)
Async XLA Ops:
  0.0 6.4 %copy-start = (f32[40,3,32,128]{3,2,1,0:T(8,128)S(1)}, f32[40,3,32,128]{3,2,1,0:T(8,128)}, u32[]{:S(2)}) copy-start(f32[40,3,32,128]{3,2,1,0:T(8,128)} %tracers.5) | copy-start | bytes 5898244
  0.0 6.4 %copy-start.1 = (f32[2,3,32,128]{3,2,1,0:T(8,128)S(1)}, f32[2,3,32,128]{3,2,1,0:T(8,128)}, u32[]{:S(2)}) copy-start(f32[2,3,32,128]{3,2,1,0:T(8,128)} %velocity.5) | copy-start | bytes 294916
  0.0 6.4 %copy-start.2 = (s32[3,32,128]{2,1,0:T(8,128)S(1)}, s32[3,32,128]{2,1,0:T(8,128)}, u32[]{:S(2)}) copy-start(s32[3,32,128]{2,1,0:T(8,128)} %mask.7) | copy-start | bytes 147460
  0.0 8.3 %copy-start.3 = (f32[32,128]{1,0:T(8,128)S(1)}, f32[32,128]{1,0:T(8,128)}, u32[]{:S(2)}) copy-start(f32[32,128]{1,0:T(8,128)} %sunlight.1) | copy-start | bytes 49156
  0.0 8.3 %copy-start.4 = (s32[10,26]{1,0:T(8,128)S(1)}, s32[10,26]{1,0:T(8,128)}, u32[]{:S(2)}) copy-start(s32[10,26]{1,0:T(8,128)} %palatable.1) | copy-start | bytes 3124
  0.0 8.3 %copy-start.5 = (f32[4,26]{1,0:T(4,128)S(1)}, f32[4,26]{1,0:T(4,128)}, u32[]{:S(2)}) copy-start(f32[4,26]{1,0:T(4,128)} %half_sat.1) | copy-start | bytes 1252
  0.0 8.3 %copy-start.6 = (f32[26]{0:T(128)S(1)}, f32[26]{0:T(128)}, u32[]{:S(2)}) copy-start(f32[26]{0:T(128)} %growth_max.1) | copy-start | bytes 316
  0.0 8.3 %copy-start.7 = (f32[26]{0:T(128)S(1)}, f32[26]{0:T(128)}, u32[]{:S(2)}) copy-start(f32[26]{0:T(128)} %light_half.1) | copy-start | bytes 316
  0.0 8.3 %copy-start.8 = (f32[10]{0:T(128)S(1)}, f32[10]{0:T(128)}, u32[]{:S(2)}) copy-start(f32[10]{0:T(128)} %graze_max.1) | copy-start | bytes 124
  0.1 8.3 %copy-start.9 = (f32[10]{0:T(128)S(1)}, f32[10]{0:T(128)}, u32[]{:S(2)}) copy-start(f32[10]{0:T(128)} %graze_half.1) | copy-start | bytes 124
  0.1 8.3 %copy-start.10 = (f32[4]{0:T(128)S(1)}, f32[4]{0:T(128)}, u32[]{:S(2)}) copy-start(f32[4]{0:T(128)} %stoichiometry.1) | copy-start | bytes 52
  1.3 9.7 %collective-permute-start.1 = (f32[248,128]{1,0:T(8,128)S(1)}, f32[248,128]{1,0:T(8,128)S(1)}, u32[]{:S(2)}, u32[]{:S(2)}) collective-permute-start(f32[248,128]{1,0:T(8,128)S(1)} %bitcast.9), channel_id=1, source_target_pairs={{4,0},{8,4},{12,8},{0,12},{5,1},{9,5},{13,9},{1,13},{6,2},{10,6},{... | collective-permute-start | bytes 380936 | tf_op jit(solution)/shard_map/ppermute | solution.py:570
  6.4 6.7 %collective-permute-start = (f32[248,128]{1,0:T(8,128)S(1)}, f32[248,128]{1,0:T(8,128)S(1)}, u32[]{:S(2)}, u32[]{:S(2)}) collective-permute-start(f32[248,128]{1,0:T(8,128)S(1)} %bitcast.8), channel_id=1, source_target_pairs={{0,4},{4,8},{8,12},{12,0},{1,5},{5,9},{9,13},{13,1},{2,6},{6,10},{... | collective-permute-start | bytes 380936 | tf_op jit(solution)/shard_map/ppermute | solution.py:569
  13.7 3.2 %collective-permute-start.2 = (f32[3,32,128]{2,1,0:T(8,128)S(1)}, f32[3,32,128]{2,1,0:T(8,128)S(1)}, u32[]{:S(2)}, u32[]{:S(2)}) collective-permute-start(f32[3,32,128]{2,1,0:T(8,128)S(1)} %get-tuple-element.27.my_first), channel_id=1, source_target_pairs={{0,1},{1,0},{2,3},{3,2},{4,5},{5,4},{6,7},{7,6},{8,9},{9,8},{10,11... | collective-permute-start | bytes 147464 | tf_op jit(solution)/shard_map/ppermute | solution.py:623
  13.8 3.6 %collective-permute-start.3 = (f32[3,32,128]{2,1,0:T(8,128)S(1)}, f32[3,32,128]{2,1,0:T(8,128)S(1)}, u32[]{:S(2)}, u32[]{:S(2)}) collective-permute-start(f32[3,32,128]{2,1,0:T(8,128)S(1)} %get-tuple-element.28.my_second), channel_id=1, source_target_pairs={{1,2},{2,1},{3,0},{0,3},{5,6},{6,5},{7,4},{4,7},{9,10},{10,9},{11,... | collective-permute-start | bytes 147464 | tf_op jit(solution)/shard_map/ppermute | solution.py:624
where the time goes:
time: 19.3 us; the launch traced here: 19.1 us
  Pallas kernels  9.45 us (49%)
  starting transfers between devices  6.81 us (35%)
  waiting for transfers between devices  2.64 us (14%)
    ppermute x1, starting transfers between devices, shards(): after = lax.ppermute(first, 'tx', down(tx))  5.14 us
    pallas_call x1, Pallas kernels, shards(): call(ecology, field, [VMEM] * 4 + [SMEM] * 6 + [VMEM], scratch=[pltpu.VME...  2.51 us
    ppermute x1, waiting for transfers between devices, shards(): before = lax.ppermute(last, 'tx', up(tx))  2.18 us
    pallas_call x1, Pallas kernels, shards(): call(interior, (field, columns, columns, stencils, ends), [VMEM] * 3, scr...  1.9 us
    pallas_call x1, Pallas kernels, shards(): call(finish, (field, jax.ShapeDtypeStruct(tracers.shape, f32)), [VMEM] *...  1.72 us
    ppermute x1, starting transfers between devices, shards(): from_second = lax.ppermute(pack_second, 'ty', turns[1])  1.59 us
    pallas_call x1, Pallas kernels, shards(): call(border_across, (field, pltpu.VMEM((PREPARED, levels, length, lanes),...  1.52 us
    pallas_call x1, Pallas kernels, shards(): call(pack_rows, (row_message, row_message), [HBM, HBM, HBM], scratch=[plt...  1.17 us
  transfers between devices with their start and end apart: 4, of which 2 were waited for; matrix products, arithmetic and copies ran while one was open for 0% of the time, Pallas kernels for 31%

commit v1 on v0

--- a/solution.py
+++ b/solution.py
@@ -496,37 +496,25 @@
             odd[level, here] = jnp.where(slot_odd, low, high)
         return carry
 
+    outer = (lane < 2) | (lane > lanes - 3)
+    step = max(n for n in (20, 10, 8, 4, 2) if count % n == 0)
+    copies = []
     for level in range(levels):
         level_step(level, 0)
-    outer = (lane < 2) | (lane > lanes - 3)
-    step = 4 if count % 4 == 0 else 2
-
-    def copy(chunk):
-        part = pl.ds(chunk * step, step)
-        return pltpu.make_async_copy(done.at[part], updated.at[part], sems.at[chunk])
-
-    def add(chunk, carry):
-        start = chunk * step
-        turns = [(lanes - 2 * (start + n)) % lanes for n in range(step)]
-        later = Deferred(2 * DEPTH)
-        for n in range(step):
-            for level in range(levels):
+        for start in range(0, count, step):
+            later = Deferred(4 * DEPTH)
+            for t in range(start, start + step):
                 for block in range(blocks):
                     here = pl.ds(8 * block, 8)
-                    edge = pltpu.roll((even, odd)[n % 2][level, here], turns[n], 1)
-                    at = (start + n, level, here)
+                    edge = pltpu.roll((even, odd)[t % 2][level, here], (lanes - 2 * t) % lanes, 1)
+                    at = (t, level, here)
                     later.put(done, at, done[at] + jnp.where(outer, edge, 0.0))
-        later.flush()
-        copy(chunk).start()
-        return carry
-
-    def wait(chunk, carry):
-        copy(chunk).wait()
-        return carry
-
-    for chunk in range(count // step):
-        add(chunk, 0)
-    lax.fori_loop(0, count // step, wait, 0)
+            later.flush()
+            part = (pl.ds(start, step), level)
+            copies.append(pltpu.make_async_copy(done.at[part], updated.at[part], sems.at[len(copies)]))
+            copies[-1].start()
+    for copy in copies:
+        copy.wait()
 
 
 def shards(

time: 19.3 us -> 19.6 us (1.016)
  Pallas kernels: 9.45 us -> 9.83 us
    pallas_call x1, Pallas kernels: 1.72 us -> 2.1 us  [shards(): call(finish, (field, jax.ShapeDtypeStruct(tracers.shape, f32)), [VMEM] *...]
  transfers between devices with their start and end apart: 4 -> 4, of which waited for: 2 -> 2; matrix products, arithmetic and copies ran while one was open for 0% -> 0% of each run, Pallas kernels for 31% -> 30%
where the time goes in v1:
time: 19.6 us; the launch traced here: 19.5 us
  Pallas kernels  9.83 us (50%)
  starting transfers between devices  6.81 us (35%)
  waiting for transfers between devices  2.64 us (13%)
    ppermute x1, starting transfers between devices, shards(): after = lax.ppermute(first, 'tx', down(tx))  5.14 us
    pallas_call x1, Pallas kernels, shards(): call(ecology, field, [VMEM] * 4 + [SMEM] * 6 + [VMEM], scratch=[pltpu.VME...  2.51 us
    ppermute x1, waiting for transfers between devices, shards(): before = lax.ppermute(last, 'tx', up(tx))  2.18 us
    pallas_call x1, Pallas kernels, shards(): call(finish, (field, jax.ShapeDtypeStruct(tracers.shape, f32)), [VMEM] *...  2.1 us
    pallas_call x1, Pallas kernels, shards(): call(interior, (field, columns, columns, stencils, ends), [VMEM] * 3, scr...  1.9 us
    ppermute x1, starting transfers between devices, shards(): from_second = lax.ppermute(pack_second, 'ty', turns[1])  1.59 us
    pallas_call x1, Pallas kernels, shards(): call(border_across, (field, pltpu.VMEM((PREPARED, levels, length, lanes),...  1.52 us
    pallas_call x1, Pallas kernels, shards(): call(pack_rows, (row_message, row_message), [HBM, HBM, HBM], scratch=[plt...  1.17 us
  transfers between devices with their start and end apart: 4, of which 2 were waited for; matrix products, arithmetic and copies ran while one was open for 0% of the time, Pallas kernels for 30%

profile of v1, /device:TPU:0, one launch (start us, length us, event | category | flops | bytes accessed | tf_op | source)
XLA Modules:
  0.0 19.5 jit_solution(17834733291795188205)
XLA Ops:
  0.0 0.0 copy-start
  0.0 0.0 copy-start.5
  0.0 0.0 copy-start.6
  0.0 0.0 copy-start.7
  0.0 0.0 copy-start.8
  0.1 0.0 copy-start.9
  0.1 0.0 copy-start.10
  0.1 1.2 %shard_map.109 = (f32[124,2,1,128]{3,2,1,0:T(1,128)S(1)}, f32[124,2,1,128]{3,2,1,0:T(1,128)S(1)}) custom-call(f32[120,32,1,128]{3,2,1,0:T(1,128)} %bitcast.5, f32[2,3,32,1,128]{4,3,2,1,0:T(1,128)} %bitcast.6, s32[3,32,1,128]{3,2,1,0:T(1,128)} %bitcast.7), custom_call_target="tpu_custom_call" | custom-call | bytes 126976 | tf_op jit(solution)/shard_map/pallas_call | solution.py:544
  1.3 5.1 %collective-permute-start.1 = (f32[248,128]{1,0:T(8,128)S(1)}, f32[248,128]{1,0:T(8,128)S(1)}, u32[]{:S(2)}, u32[]{:S(2)}) collective-permute-start(f32[248,128]{1,0:T(8,128)S(1)} %bitcast.9), channel_id=1, source_target_pairs={{4,0},{8,4},{12,8},{0,12},{5,1},{9,5},{13,9},{1,13},{6,2},{10,6},{... | collective-permute-start | bytes 380936 | tf_op jit(solution)/shard_map/ppermute | solution.py:558
  6.4 0.0 collective-permute-start
  6.4 0.0 copy-done
  6.4 0.0 copy-done.1
  6.4 0.0 copy-done.2
  6.4 1.9 %shard_map.110 = (f32[40,3,32,128]{3,2,1,0:T(8,128)S(1)}, f32[3,32,128]{2,1,0:T(8,128)S(1)}, f32[3,32,128]{2,1,0:T(8,128)S(1)}, f32[5,3,32,128]{3,2,1,0:T(8,128)S(1)}, f32[40,3,16,128]{3,2,1,0:T(8,128)S(1)}) custom-call(f32[40,3,32,128]{3,2,1,0:T(8,128)S(1)} %copy-done, f32[2,3,32,128]{3,2,1,0:T(8,128)S(1)} %copy-done.1, s32[3,32,128]{2,1,0:T(8,128)S(1)} %copy-done.2), custom_call_target="tpu_custom_call" | custom-call | flops 9830400 | bytes 3932160 | tf_op jit(solution)/shard_map/pallas_call | solution.py:565
  8.3 0.0 copy-done.3
  8.3 0.0 copy-done.4
  8.3 0.0 copy-done.5
  8.4 0.0 copy-done.6
  8.4 0.0 copy-done.7
  8.4 0.0 copy-done.8
  8.4 0.0 copy-done.9
  8.4 0.0 copy-done.10
  8.4 2.5 %shard_map.111._partial = f32[40,3,32,128]{3,2,1,0:T(8,128)S(1)} custom-call(f32[40,3,32,128]{3,2,1,0:T(8,128)S(1)} %copy-done, s32[3,32,128]{2,1,0:T(8,128)S(1)} %copy-done.2, f32[32,128]{1,0:T(8,128)S(1)} %copy-done.3, s32[10,26]{1,0:T(8,128)S(1)} %copy-done.4, f32[26]{0:T(128)S(1)} %copy-done.6, ...), custom_call_target="tpu_custom_call", output_to_operand_aliasing={{}: (10, {})} | custom-call | flops 19660800 | bytes 3932160 | tf_op jit(solution)/shard_map/pallas_call | solution.py:574
  10.9 0.0 collective-permute-done.1.after
  10.9 2.2 %collective-permute-done.before = f32[248,128]{1,0:T(8,128)S(1)} collective-permute-done((f32[248,128]{1,0:T(8,128)S(1)}, f32[248,128]{1,0:T(8,128)S(1)}, u32[]{:S(2)}, u32[]{:S(2)}) %collective-permute-start) | collective-permute-done | bytes 127008 | tf_op jit(solution)/shard_map/ppermute | solution.py:557
  13.1 0.6 %shard_map.112 = (f32[40,3,16,128]{3,2,1,0:T(8,128)S(1)}, f32[3,32,128]{2,1,0:T(8,128)S(1)}, f32[3,32,128]{2,1,0:T(8,128)S(1)}, f32[40,3,32,128]{3,2,1,0:T(8,128)S(1)}) custom-call(f32[40,3,32,128]{3,2,1,0:T(8,128)S(1)} %copy-done, f32[2,3,32,128]{3,2,1,0:T(8,128)S(1)} %copy-done.1, ...), custom_call_target="tpu_custom_call", output_to_operand_aliasing={{3}: (5, {}), {1}: (6, {}), {2}: (7, {}), {0}: (8, {})} | custom-call | flops 4915200 | bytes 3932160 | tf_op jit(solution)/shard_map/pallas_call | solution.py:599
  13.7 0.1 collective-permute-start.2
  13.8 1.6 %collective-permute-start.3 = (f32[3,32,128]{2,1,0:T(8,128)S(1)}, f32[3,32,128]{2,1,0:T(8,128)S(1)}, u32[]{:S(2)}, u32[]{:S(2)}) collective-permute-start(f32[3,32,128]{2,1,0:T(8,128)S(1)} %get-tuple-element.28.my_second), channel_id=1, source_target_pairs={{1,2},{2,1},{3,0},{0,3},{5,6},{6,5},{7,4},{4,7},{9,10},{10,9},{11,... | collective-permute-start | bytes 147464 | tf_op jit(solution)/shard_map/ppermute | solution.py:612
  15.4 1.5 %shard_map.113 = (f32[40,3,32,128]{3,2,1,0:T(8,128)S(1)}, f32[8,3,32,128]{3,2,1,0:T(8,128)S(1)}) custom-call(f32[40,3,16,128]{3,2,1,0:T(8,128)S(1)} %get-tuple-element.25.swept, f32[2,3,32,128]{3,2,1,0:T(8,128)S(1)} %copy-done.1, s32[3,32,128]{2,1,0:T(8,128)S(1)} %copy-done.2, ...), custom_call_target="tpu_custom_call", output_to_operand_aliasing={{0}: (6, {})} | custom-call | flops 4915200 | bytes 2949120 | tf_op jit(solution)/shard_map/pallas_call | solution.py:613
  16.9 0.0 collective-permute-done.2.first
  16.9 0.5 %collective-permute-done.3.second = f32[3,32,128]{2,1,0:T(8,128)S(1)} collective-permute-done((f32[3,32,128]{2,1,0:T(8,128)S(1)}, f32[3,32,128]{2,1,0:T(8,128)S(1)}, u32[]{:S(2)}, u32[]{:S(2)}) %collective-permute-start.3) | collective-permute-done | bytes 49184 | tf_op jit(solution)/shard_map/ppermute | solution.py:612
  17.4 2.1 %shard_map.114 = (f32[40,3,32,128]{3,2,1,0:T(8,128)S(1)}, f32[40,3,32,128]{3,2,1,0:T(8,128)}) custom-call(f32[8,3,32,128]{3,2,1,0:T(8,128)S(1)} %get-tuple-element.30.ready, f32[3,32,128]{2,1,0:T(8,128)S(1)} %collective-permute-done.2.first, f32[3,32,128]{2,1,0:T(8,128)S(1)} %collective-permute-done.3.second, ...), custom_call_target="tpu_custom_call", output_to_operand_aliasing={{0}: (3, {})} | custom-call | flops 1966080 | bytes 3932160 | tf_op jit(solution)/shard_map/pallas_call | solution.py:622
  (4 shorter events, 0.0 us)
Async XLA Ops:
  0.0 6.4 %copy-start = (f32[40,3,32,128]{3,2,1,0:T(8,128)S(1)}, f32[40,3,32,128]{3,2,1,0:T(8,128)}, u32[]{:S(2)}) copy-start(f32[40,3,32,128]{3,2,1,0:T(8,128)} %tracers.5) | copy-start | bytes 5898244
  0.0 6.4 %copy-start.1 = (f32[2,3,32,128]{3,2,1,0:T(8,128)S(1)}, f32[2,3,32,128]{3,2,1,0:T(8,128)}, u32[]{:S(2)}) copy-start(f32[2,3,32,128]{3,2,1,0:T(8,128)} %velocity.5) | copy-start | bytes 294916
  0.0 6.4 %copy-start.2 = (s32[3,32,128]{2,1,0:T(8,128)S(1)}, s32[3,32,128]{2,1,0:T(8,128)}, u32[]{:S(2)}) copy-start(s32[3,32,128]{2,1,0:T(8,128)} %mask.7) | copy-start | bytes 147460
  0.0 8.3 %copy-start.3 = (f32[32,128]{1,0:T(8,128)S(1)}, f32[32,128]{1,0:T(8,128)}, u32[]{:S(2)}) copy-start(f32[32,128]{1,0:T(8,128)} %sunlight.1) | copy-start | bytes 49156
  0.0 8.3 %copy-start.4 = (s32[10,26]{1,0:T(8,128)S(1)}, s32[10,26]{1,0:T(8,128)}, u32[]{:S(2)}) copy-start(s32[10,26]{1,0:T(8,128)} %palatable.1) | copy-start | bytes 3124
  0.0 8.3 %copy-start.5 = (f32[4,26]{1,0:T(4,128)S(1)}, f32[4,26]{1,0:T(4,128)}, u32[]{:S(2)}) copy-start(f32[4,26]{1,0:T(4,128)} %half_sat.1) | copy-start | bytes 1252
  0.0 8.3 %copy-start.6 = (f32[26]{0:T(128)S(1)}, f32[26]{0:T(128)}, u32[]{:S(2)}) copy-start(f32[26]{0:T(128)} %growth_max.1) | copy-start | bytes 316
  0.0 8.3 %copy-start.7 = (f32[26]{0:T(128)S(1)}, f32[26]{0:T(128)}, u32[]{:S(2)}) copy-start(f32[26]{0:T(128)} %light_half.1) | copy-start | bytes 316
  0.0 8.3 %copy-start.8 = (f32[10]{0:T(128)S(1)}, f32[10]{0:T(128)}, u32[]{:S(2)}) copy-start(f32[10]{0:T(128)} %graze_max.1) | copy-start | bytes 124
  0.1 8.3 %copy-start.9 = (f32[10]{0:T(128)S(1)}, f32[10]{0:T(128)}, u32[]{:S(2)}) copy-start(f32[10]{0:T(128)} %graze_half.1) | copy-start | bytes 124
  0.1 8.3 %copy-start.10 = (f32[4]{0:T(128)S(1)}, f32[4]{0:T(128)}, u32[]{:S(2)}) copy-start(f32[4]{0:T(128)} %stoichiometry.1) | copy-start | bytes 52
  1.3 9.7 %collective-permute-start.1 = (f32[248,128]{1,0:T(8,128)S(1)}, f32[248,128]{1,0:T(8,128)S(1)}, u32[]{:S(2)}, u32[]{:S(2)}) collective-permute-start(f32[248,128]{1,0:T(8,128)S(1)} %bitcast.9), channel_id=1, source_target_pairs={{4,0},{8,4},{12,8},{0,12},{5,1},{9,5},{13,9},{1,13},{6,2},{10,6},{... | collective-permute-start | bytes 380936 | tf_op jit(solution)/shard_map/ppermute | solution.py:558
  6.4 6.7 %collective-permute-start = (f32[248,128]{1,0:T(8,128)S(1)}, f32[248,128]{1,0:T(8,128)S(1)}, u32[]{:S(2)}, u32[]{:S(2)}) collective-permute-start(f32[248,128]{1,0:T(8,128)S(1)} %bitcast.8), channel_id=1, source_target_pairs={{0,4},{4,8},{8,12},{12,0},{1,5},{5,9},{9,13},{13,1},{2,6},{6,10},{... | collective-permute-start | bytes 380936 | tf_op jit(solution)/shard_map/ppermute | solution.py:557
  13.7 3.2 %collective-permute-start.2 = (f32[3,32,128]{2,1,0:T(8,128)S(1)}, f32[3,32,128]{2,1,0:T(8,128)S(1)}, u32[]{:S(2)}, u32[]{:S(2)}) collective-permute-start(f32[3,32,128]{2,1,0:T(8,128)S(1)} %get-tuple-element.27.my_first), channel_id=1, source_target_pairs={{0,1},{1,0},{2,3},{3,2},{4,5},{5,4},{6,7},{7,6},{8,9},{9,8},{10,11... | collective-permute-start | bytes 147464 | tf_op jit(solution)/shard_map/ppermute | solution.py:611
  13.8 3.6 %collective-permute-start.3 = (f32[3,32,128]{2,1,0:T(8,128)S(1)}, f32[3,32,128]{2,1,0:T(8,128)S(1)}, u32[]{:S(2)}, u32[]{:S(2)}) collective-permute-start(f32[3,32,128]{2,1,0:T(8,128)S(1)} %get-tuple-element.28.my_second), channel_id=1, source_target_pairs={{1,2},{2,1},{3,0},{0,3},{5,6},{6,5},{7,4},{4,7},{9,10},{10,9},{11,... | collective-permute-start | bytes 147464 | tf_op jit(solution)/shard_map/ppermute | solution.py:612
